TPU v7x, 128 devices: a whole 4x4x4 slice. The times are simulated.
128 devices in a mesh: row: 8 (over x_lo, y), col: 16 (over x_hi, z, core).
Axes of the slice: x: 4 (x_hi: 2, x_lo: 2; x = x_hi * 2 + x_lo), y: 4, z: 4, core: 2. Of those that a mesh axis runs over, the one named last changes fastest.
Arguments:
- features: bfloat16 [262144, 256], P(('col', 'row')), may hold values from -6 to 6
- weight: bfloat16 [256, 256], replicated, may hold values from -0.375 to 0.375
- adj_rows: int32 [8, 16, 128], P('row', 'col'), may hold values from 0 to 255, as said below
- adj_cols: int32 [8, 16, 128], P('row', 'col'), may hold values from 0 to 127
- adj_blocks: bfloat16 [8, 16, 128, 128, 128], P('row', 'col'), as said below
- counts: int32 [8, 16], P('row', 'col'), may hold values from 1 to 128, as said below
- grad_out: bfloat16 [262144, 256], P(('col', 'row')), may hold values from -6 to 6
Outputs:
- out_col: bfloat16 [262144, 256], P(('col', 'row'))
- weight_grad: float32 [256, 256], replicated
Inputs may be any that keep to these rules, and one draw needn't show every extreme that they name: `adj_rows`: in every grid cell, slot k's block-row lies in [(k % 16) * 16, (k % 16 + 1) * 16), and no two slots of a cell share a block-row. At least one grid cell has all 128 slots live; live slots are the first counts of a cell. `adj_blocks`: each block holds nonnegative edge weights.
All inputs are finite; a program needn't handle non-finite values.
Results may differ from a plain program's by a relative error of at most 0.015.
Values may be sent and summed in bfloat16 or wider, within the bound.
No kernel may reach another device: no remote copies, remote signals or barrier semaphores. Data moves between devices by JAX's collectives and lax.ppermute only.
A program may use at most 128 MiB of HBM per device.

v0:
```python
import jax
import jax.numpy as jnp
from jax import lax
from jax.sharding import PartitionSpec as P

VBLK = 16


def group_products(col_blocks, slab_cols, blocks, live_count, first_slot, group):
    cols_here = lax.dynamic_slice_in_dim(slab_cols, first_slot, group)
    blocks_here = lax.dynamic_slice_in_dim(blocks, first_slot, group, 0)
    live_mask = first_slot + jnp.arange(group) < live_count
    picked = col_blocks[cols_here]
    products = jnp.einsum("kil,klf->kif", blocks_here, picked, preferred_element_type=jnp.float32)
    return jnp.where(live_mask[:, None, None], products, 0.0).astype(jnp.bfloat16)


def dense_partial(col_blocks, slab_rows, slab_cols, blocks, live_count, row_blocks, group):
    block_size = blocks.shape[-1]
    feat_width = col_blocks.shape[-1]
    turns = (live_count + group - 1) // group

    def one_group(group_idx, running):
        first_slot = group_idx * group
        rows_here = lax.dynamic_slice_in_dim(slab_rows, first_slot, group)
        products = group_products(col_blocks, slab_cols, blocks, live_count, first_slot, group)
        return running.at[rows_here].add(products)

    start_value = jnp.zeros((row_blocks, block_size, feat_width), jnp.bfloat16)
    running = lax.fori_loop(0, turns, one_group, start_value)
    return running.reshape(row_blocks * block_size, feat_width)


def derivative(preact, grad_rows):
    sigmoid_pre = jax.nn.sigmoid(preact)
    return (
        grad_rows.astype(jnp.float32) * sigmoid_pre * (1.0 + preact * (1.0 - sigmoid_pre))
    ).astype(jnp.bfloat16)


def on_device(features, weight, adj_rows, adj_cols, adj_blocks, counts, grad_out):
    feat_width = features.shape[1]
    local_rows = features.shape[0]
    owners = lax.axis_size("col")
    devices_all = lax.axis_size("row") * owners
    piece_rows = local_rows // devices_all
    block_size = adj_blocks.shape[-1]
    slot_total = adj_blocks.shape[2]
    group = min(32, slot_total)
    row_blocks = VBLK * owners
    slab = lax.all_gather(features, "row", axis=0, tiled=True)
    col_blocks = slab.reshape(-1, block_size, feat_width)
    slab_rows = adj_rows[0, 0]
    slab_cols = adj_cols[0, 0]
    blocks = adj_blocks[0, 0]
    live_count = counts[0, 0]
    partial_value = dense_partial(
        col_blocks, slab_rows, slab_cols, blocks, live_count, row_blocks, group
    )
    agg = (
        lax.psum_scatter(partial_value, "col", scatter_dimension=0, tiled=True)
        .astype(jnp.float32)
        .astype(jnp.bfloat16)
    )
    preact = jnp.dot(agg, weight, preferred_element_type=jnp.float32)
    out_row = jax.nn.silu(preact).astype(jnp.bfloat16)
    contract = (((0,), (0,)), ((), ()))
    moved = lax.all_to_all(
        out_row.reshape(devices_all, piece_rows, feat_width),
        ("row", "col"),
        split_axis=0,
        concat_axis=0,
        tiled=True,
    )
    out_col = moved.reshape(local_rows, feat_width)
    grad_row = lax.all_to_all(
        grad_out.reshape(devices_all, piece_rows, feat_width),
        ("row", "col"),
        split_axis=0,
        concat_axis=0,
        tiled=True,
    )
    grad_pre = derivative(preact, grad_row.reshape(local_rows, feat_width))
    weight_part = lax.dot_general(agg, grad_pre, contract, preferred_element_type=jnp.float32)
    weight_grad = lax.psum(weight_part, ("row", "col")) * (local_rows * devices_all) ** (-0.5)
    return (out_col, weight_grad)


def solution(mesh):
    placed = (
        P(("col", "row"), None),
        P(),
        P("row", "col", None),
        P("row", "col", None),
        P("row", "col", None, None, None),
        P("row", "col"),
        P(("col", "row"), None),
    )
    return jax.shard_map(
        on_device,
        mesh=mesh,
        in_specs=placed,
        out_specs=(P(("col", "row"), None), P()),
        check_vma=False,
    )
```

profile of v0, /device:TPU:1, one launch (start us, length us, event | category | flops | bytes accessed | tf_op | source)
XLA Modules:
  0.0 496.6 jit_solution(323156815200104506)
XLA Ops:
  7.2 0.0 copy-start
  7.2 0.0 all-gather.2.cloned.1.call-start
  7.2 0.7 all-gather.2.cloned.1.call-update
  7.9 0.0 reduce-scatter.2.cloned.1.call-start
  8.6 96.2 %all-gather.2.cloned.1.call-done = bf16[16384,256]{1,0:T(8,128)(2,1)} async-done(((bf16[2048,256]{1,0:T(8,128)(2,1)}), bf16[16384,256]{1,0:T(8,128)(2,1)}) %all-gather.2.cloned.1.call-update) | async-done | bytes 8388624 | tf_op jit(solution)/shard_map/all_gather | solution.py:51
  104.8 0.0 copy-start.3
  104.8 0.0 copy-start.4
  104.8 6.0 %broadcast_in_dim.22 = bf16[256,128,256]{2,1,0:T(8,128)(2,1)} broadcast(bf16[]{:T(256)} %constant.35.clone.1), dimensions={} | broadcast | bytes 16777218 | tf_op jit(solution)/shard_map/broadcast_in_dim | solution.py:29
  110.8 0.0 copy-done.3
  110.8 0.0 copy-done.4
  110.8 72.3 %while.10 = (s32[]{:T(128)}, bf16[256,128,256]{2,1,0:T(8,128)(2,1)}, s32[]{:T(128)}, s32[128]{0:T(128)S(1)}, s32[]{:T(128)}, /*index=5*/bf16[128,128,128]{2,1,0:...) while((s32[]{:T(128)}, ...), condition=%wide.region_2.3_spmd, body=%wide.region_0.2_spmd.sunk | while | flops 271582464 | bytes 15733875 | solution.py:30
  110.8 0.1 compare_select_fusion.3
  110.9 5.4 %gather_fusion = bf16[32,128,256]{2,1,0:T(8,128)(2,1)} fusion(bf16[128,128,256]{2,1,0:T(8,128)(2,1)} %get-tuple-element.151, s32[1024]{0:T(1024)S(1)} %pad_clamp_fusion.2), kind=kCustom, calls=%fused_computation.clone.1 | custom fusion | bytes 4194432 | tf_op jit(solution)/shard_map/while/body/gather | solution.py:13
  116.3 0.7 add_compare_fusion.2
  117.0 2.6 select_convert_fusion.2
  119.6 9.3 %scatter_fusion = bf16[256,128,256]{2,1,0:T(8,128)(2,1)} fusion(bf16[256,128,256]{2,1,0:T(8,128)(2,1)} %get-tuple-element.133, s32[32]{0:T(128)S(1)} %get-tuple-element.118, bf16[32,128,256]{2,1,0:T(8,128)(2,1)S(1)} %select_convert_fusion.2), kind=kCustom, calls=%fused_computation.1.clone.1 | custom fusion | flops 1048576 | bytes 6291584 | tf_op jit(solution)/shard_map/while/body/scatter-add | solution.py:27
  128.9 0.1 compare_select_fusion.3
  129.0 5.4 %gather_fusion = bf16[32,128,256]{2,1,0:T(8,128)(2,1)} fusion(bf16[128,128,256]{2,1,0:T(8,128)(2,1)} %get-tuple-element.151, s32[1024]{0:T(1024)S(1)} %pad_clamp_fusion.2), kind=kCustom, calls=%fused_computation.clone.1 | custom fusion | bytes 4194432 | tf_op jit(solution)/shard_map/while/body/gather | solution.py:13
  134.4 0.7 add_compare_fusion.2
  135.1 2.6 select_convert_fusion.2
  137.7 9.3 %scatter_fusion = bf16[256,128,256]{2,1,0:T(8,128)(2,1)} fusion(bf16[256,128,256]{2,1,0:T(8,128)(2,1)} %get-tuple-element.133, s32[32]{0:T(128)S(1)} %get-tuple-element.118, bf16[32,128,256]{2,1,0:T(8,128)(2,1)S(1)} %select_convert_fusion.2), kind=kCustom, calls=%fused_computation.1.clone.1 | custom fusion | flops 1048576 | bytes 6291584 | tf_op jit(solution)/shard_map/while/body/scatter-add | solution.py:27
  147.0 0.1 compare_select_fusion.3
  147.1 5.4 %gather_fusion = bf16[32,128,256]{2,1,0:T(8,128)(2,1)} fusion(bf16[128,128,256]{2,1,0:T(8,128)(2,1)} %get-tuple-element.151, s32[1024]{0:T(1024)S(1)} %pad_clamp_fusion.2), kind=kCustom, calls=%fused_computation.clone.1 | custom fusion | bytes 4194432 | tf_op jit(solution)/shard_map/while/body/gather | solution.py:13
  152.5 0.7 add_compare_fusion.2
  153.1 2.6 select_convert_fusion.2
  155.8 9.3 %scatter_fusion = bf16[256,128,256]{2,1,0:T(8,128)(2,1)} fusion(bf16[256,128,256]{2,1,0:T(8,128)(2,1)} %get-tuple-element.133, s32[32]{0:T(128)S(1)} %get-tuple-element.118, bf16[32,128,256]{2,1,0:T(8,128)(2,1)S(1)} %select_convert_fusion.2), kind=kCustom, calls=%fused_computation.1.clone.1 | custom fusion | flops 1048576 | bytes 6291584 | tf_op jit(solution)/shard_map/while/body/scatter-add | solution.py:27
  165.1 0.1 compare_select_fusion.3
  165.2 5.4 %gather_fusion = bf16[32,128,256]{2,1,0:T(8,128)(2,1)} fusion(bf16[128,128,256]{2,1,0:T(8,128)(2,1)} %get-tuple-element.151, s32[1024]{0:T(1024)S(1)} %pad_clamp_fusion.2), kind=kCustom, calls=%fused_computation.clone.1 | custom fusion | bytes 4194432 | tf_op jit(solution)/shard_map/while/body/gather | solution.py:13
  170.6 0.7 add_compare_fusion.2
  171.2 2.6 select_convert_fusion.2
  173.9 9.2 %scatter_fusion = bf16[256,128,256]{2,1,0:T(8,128)(2,1)} fusion(bf16[256,128,256]{2,1,0:T(8,128)(2,1)} %get-tuple-element.133, s32[32]{0:T(128)S(1)} %get-tuple-element.118, bf16[32,128,256]{2,1,0:T(8,128)(2,1)S(1)} %select_convert_fusion.2), kind=kCustom, calls=%fused_computation.1.clone.1 | custom fusion | flops 1048576 | bytes 6291584 | tf_op jit(solution)/shard_map/while/body/scatter-add | solution.py:27
  183.1 0.0 copy-start.1
  183.1 0.0 reduce-scatter.2.cloned.1.call-update
  183.1 1.2 copy-done.1
  184.3 26.0 %all_to_all.10 = bf16[128,16,256]{2,1,0:T(8,128)(2,1)S(1)} all-to-all(bf16[128,16,256]{2,1,0:T(8,128)(2,1)S(1)} %bitcast.24), channel_id=1, replica_groups=mesh['row'=8,'col'=16] {'row','col'}, dimensions={0} | all-to-all | bytes 2097152 | tf_op jit(solution)/shard_map/all_to_all | solution.py:76
  210.3 117.8 %reduce-scatter.2.cloned.1.call-done = bf16[2048,256]{1,0:T(8,128)(2,1)} async-done(((bf16[32768,256]{1,0:T(8,128)(2,1)}), bf16[2048,256]{1,0:T(8,128)(2,1)}) %reduce-scatter.2.cloned.1.call-update) | async-done | bytes 1048592 | tf_op jit(solution)/shard_map/reduce_scatter | solution.py:61
  328.1 0.0 copy-done
  328.1 3.4 fusion.3
  331.5 0.0 copy-start.2
  331.5 6.7 %all-to-all-start = ((bf16[128,16,256]{2,1,0:T(8,128)(2,1)}), bf16[128,16,256]{2,1,0:T(8,128)(2,1)S(1)}, u32[]{:S(2)}, u32[]{:S(2)}) async-start(bf16[128,16,256]{2,1,0:T(8,128)(2,1)} %bitcast.6), calls=%async_computation.1 | async-start | bytes 2097152 | tf_op jit(solution)/shard_map/all_to_all | solution.py:68
  338.2 0.0 all-reduce.2.cloned.1.call-start
  338.2 0.0 copy-done.2
  338.2 1.2 fusion.4
  339.4 0.0 all-reduce.2.cloned.1.call-update
  339.4 148.0 %all-reduce.2.cloned.1.call-done = f32[256,256]{1,0:T(8,128)} async-done(((f32[256,256]{1,0:T(8,128)}), f32[256,256]{1,0:T(8,128)}) %all-reduce.2.cloned.1.call-update) | async-done | bytes 262160 | tf_op jit(solution)/shard_map/psum | solution.py:85
  487.4 1.7 broadcast_multiply_fusion
  489.1 0.0 all-to-all-done
  489.1 1.0 copy.19
  (4 shorter events, 0.0 us)
Async XLA Ops:
  7.2 321.0 %copy-start = (bf16[256,256]{1,0:T(8,128)(2,1)S(1)}, bf16[256,256]{1,0:T(8,128)(2,1)}, u32[]{:S(2)}) copy-start(bf16[256,256]{1,0:T(8,128)(2,1)} %param.10) | copy-start | bytes 393220
  7.2 97.6 %all-gather.2.cloned.1.call-start = ((), (), s32[]{:S(2)}) async-start(), calls=%async_computation.3 | async-start | bytes 9437184 | tf_op jit(solution)/shard_map/all_gather | solution.py:51
  7.9 320.2 %reduce-scatter.2.cloned.1.call-start = ((), (), s32[]{:S(2)}) async-start(), calls=%async_computation.4 | async-start | bytes 17825792 | tf_op jit(solution)/shard_map/reduce_scatter | solution.py:61
  104.8 6.0 %copy-start.3 = (s32[1,1,128]{2,1,0:T(1,128)S(1)}, s32[1,1,128]{2,1,0:T(1,128)}, u32[]{:S(2)}) copy-start(s32[1,1,128]{2,1,0:T(1,128)} %param.11) | copy-start | bytes 1540
  104.8 6.0 %copy-start.4 = (s32[1,1,128]{2,1,0:T(1,128)S(1)}, s32[1,1,128]{2,1,0:T(1,128)}, u32[]{:S(2)}) copy-start(s32[1,1,128]{2,1,0:T(1,128)} %param.12) | copy-start | bytes 1540
  183.1 1.2 copy-start.1
  331.5 6.7 %copy-start.2 = (bf16[2048,256]{1,0:T(8,128)(2,1)S(1)}, bf16[2048,256]{1,0:T(8,128)(2,1)}, u32[]{:S(2)}) copy-start(bf16[2048,256]{1,0:T(8,128)(2,1)} %reduce-scatter.2.cloned.1.call-done) | copy-start | bytes 3145732
  331.5 157.6 %all-to-all-start = ((bf16[128,16,256]{2,1,0:T(8,128)(2,1)}), bf16[128,16,256]{2,1,0:T(8,128)(2,1)S(1)}, u32[]{:S(2)}, u32[]{:S(2)}) async-start(bf16[128,16,256]{2,1,0:T(8,128)(2,1)} %bitcast.6), calls=%async_computation.1 | async-start | bytes 2097152 | tf_op jit(solution)/shard_map/all_to_all | solution.py:68
  338.2 149.3 %all-reduce.2.cloned.1.call-start = ((), (), s32[]{:S(2)}) async-start(), calls=%async_computation.5 | async-start | bytes 524288 | tf_op jit(solution)/shard_map/psum | solution.py:85
Sparse Core Ops, SparseCore 0:
  9.7 95.1 all-gather.1
  183.3 144.8 reduce-scatter.1
  344.3 143.0 all-reduce.1
where the time goes:
time: 498 us; the launch traced here: 497 us
  waiting for transfers between devices  363 us (73%)
  other arithmetic  41.8 us (8%)
  local copies, waits for them, and re-layouts  29.9 us (6%)
  blocking collectives  26 us (5%)
  matrix products  15 us (3%)
  between operations  14.4 us (3%)
  starting transfers between devices  6.78 us (1%)
    psum x1, waiting for transfers between devices, on_device(): lax.psum(weight_part, ('row', 'col')) * (local_rows * devices_all) ** (-0.5)  148 us
    reduce_scatter x1, waiting for transfers between devices, on_device(): lax.psum_scatter(partial_value, 'col', scatter_dimension=0, tiled=True)  118 us
    all_gather x1, waiting for transfers between devices, on_device(): slab = lax.all_gather(features, 'row', axis=0, tiled=True)  96.2 us
    scatter-add x4, other arithmetic, one_group(): return running.at[rows_here].add(products)  37.2 us
    all_to_all x1, blocking collectives, on_device(): lax.all_to_all(grad_out.reshape(devices_all, piece_rows, feat_width), ('r...  26 us
    gather x4, local copies, waits for them, and re-layouts, group_products(): picked = col_blocks[cols_here]  21.7 us
    dot_general x4, matrix products, group_products(): jnp.einsum('kil,klf->kif', blocks_here, picked, preferred_element_type=jn...  10.5 us
  transfers between devices with their start and end apart: 4, of which 3 were waited for; matrix products, arithmetic and copies ran while one was open for 1% of the time, Pallas kernels for 0%

commit v1 on v0

--- a/solution.py
+++ b/solution.py
@@ -1,9 +1,19 @@
+import functools
 import jax
 import jax.numpy as jnp
 from jax import lax
 from jax.sharding import PartitionSpec as P
 
 VBLK = 16
+
+
+def view_space(view, along_axis, device_axis):
+    for m in (along_axis, device_axis):
+        view = lax.psum(view, m)
+    return view
+
+
+store_points = functools.partial(view_space, along_axis="row", device_axis="col")
 
 
 def group_products(col_blocks, slab_cols, blocks, live_count, first_slot, group):
@@ -82,7 +92,7 @@
     )
     grad_pre = derivative(preact, grad_row.reshape(local_rows, feat_width))
     weight_part = lax.dot_general(agg, grad_pre, contract, preferred_element_type=jnp.float32)
-    weight_grad = lax.psum(weight_part, ("row", "col")) * (local_rows * devices_all) ** (-0.5)
+    weight_grad = store_points(weight_part) * (local_rows * devices_all) ** (-0.5)
     return (out_col, weight_grad)
 
 

time: 498 us -> 568 us (1.14)
  waiting for transfers between devices: 363 us -> 433 us
    psum x1 -> x2, waiting for transfers between devices: 148 us -> 218 us  [view_space(): view = lax.psum(view, m)]
  transfers between devices with their start and end apart: 4 -> 5, of which waited for: 3 -> 4; matrix products, arithmetic and copies ran while one was open for 1% -> 1% of each run, Pallas kernels for 0% -> 0%
where the time goes in v1:
time: 568 us; the launch traced here: 567 us
  waiting for transfers between devices  433 us (76%)
  other arithmetic  41.8 us (7%)
  local copies, waits for them, and re-layouts  29.9 us (5%)
  blocking collectives  26 us (5%)
  matrix products  15 us (3%)
  between operations  14.5 us (3%)
  starting transfers between devices  6.83 us (1%)
    psum x2, waiting for transfers between devices, view_space(): view = lax.psum(view, m)  218 us
    reduce_scatter x1, waiting for transfers between devices, on_device(): lax.psum_scatter(partial_value, 'col', scatter_dimension=0, tiled=True)  118 us
    all_gather x1, waiting for transfers between devices, on_device(): slab = lax.all_gather(features, 'row', axis=0, tiled=True)  96.2 us
    scatter-add x4, other arithmetic, one_group(): return running.at[rows_here].add(products)  37.2 us
    all_to_all x1, blocking collectives, on_device(): lax.all_to_all(grad_out.reshape(devices_all, piece_rows, feat_width), ('r...  26 us
    gather x4, local copies, waits for them, and re-layouts, group_products(): picked = col_blocks[cols_here]  21.7 us
  transfers between devices with their start and end apart: 5, of which 4 were waited for; matrix products, arithmetic and copies ran while one was open for 1% of the time, Pallas kernels for 0%

profile of v1, /device:TPU:1, one launch (start us, length us, event | category | flops | bytes accessed | tf_op | source)
XLA Modules:
  0.0 566.5 jit_solution(4875075800408725251)
XLA Ops:
  7.2 0.0 copy-start
  7.2 0.0 all-gather.2.cloned.1.call-start
  7.2 0.7 all-gather.2.cloned.1.call-update
  7.9 0.0 reduce-scatter.2.cloned.1.call-start
  8.6 96.2 %all-gather.2.cloned.1.call-done = bf16[16384,256]{1,0:T(8,128)(2,1)} async-done(((bf16[2048,256]{1,0:T(8,128)(2,1)}), bf16[16384,256]{1,0:T(8,128)(2,1)}) %all-gather.2.cloned.1.call-update) | async-done | bytes 8388624 | tf_op jit(solution)/shard_map/all_gather | solution.py:61
  104.8 0.0 copy-start.3
  104.8 6.0 %broadcast_in_dim.22 = bf16[256,128,256]{2,1,0:T(8,128)(2,1)} broadcast(bf16[]{:T(256)} %constant.35.clone.1), dimensions={} | broadcast | bytes 16777218 | tf_op jit(solution)/shard_map/broadcast_in_dim | solution.py:39
  110.8 0.0 copy-done.3
  110.8 0.0 copy-done.4
  110.8 72.3 %while.10 = (s32[]{:T(128)}, bf16[256,128,256]{2,1,0:T(8,128)(2,1)}, s32[]{:T(128)}, s32[128]{0:T(128)S(1)}, s32[]{:T(128)}, /*index=5*/bf16[128,128,128]{2,1,0:...) while((s32[]{:T(128)}, ...), condition=%wide.region_2.3_spmd, body=%wide.region_0.2_spmd.sunk | while | flops 271582464 | bytes 15733875 | solution.py:40
  110.8 0.1 compare_select_fusion.3
  110.9 5.4 gather_fusion
  116.3 0.7 add_compare_fusion.2
  117.0 2.6 select_convert_fusion.2
  119.6 9.3 %scatter_fusion = bf16[256,128,256]{2,1,0:T(8,128)(2,1)} fusion(bf16[256,128,256]{2,1,0:T(8,128)(2,1)} %get-tuple-element.133, s32[32]{0:T(128)S(1)} %get-tuple-element.118, bf16[32,128,256]{2,1,0:T(8,128)(2,1)S(1)} %select_convert_fusion.2), kind=kCustom, calls=%fused_computation.1.clone.1 | custom fusion | flops 1048576 | bytes 6291584 | tf_op jit(solution)/shard_map/while/body/scatter-add | solution.py:37
  128.9 0.1 compare_select_fusion.3
  129.0 5.4 gather_fusion
  134.4 0.7 add_compare_fusion.2
  135.1 2.6 select_convert_fusion.2
  137.7 9.3 %scatter_fusion = bf16[256,128,256]{2,1,0:T(8,128)(2,1)} fusion(bf16[256,128,256]{2,1,0:T(8,128)(2,1)} %get-tuple-element.133, s32[32]{0:T(128)S(1)} %get-tuple-element.118, bf16[32,128,256]{2,1,0:T(8,128)(2,1)S(1)} %select_convert_fusion.2), kind=kCustom, calls=%fused_computation.1.clone.1 | custom fusion | flops 1048576 | bytes 6291584 | tf_op jit(solution)/shard_map/while/body/scatter-add | solution.py:37
  147.0 0.1 compare_select_fusion.3
  147.1 5.4 gather_fusion
  152.5 0.7 add_compare_fusion.2
  153.1 2.6 select_convert_fusion.2
  155.8 9.3 %scatter_fusion = bf16[256,128,256]{2,1,0:T(8,128)(2,1)} fusion(bf16[256,128,256]{2,1,0:T(8,128)(2,1)} %get-tuple-element.133, s32[32]{0:T(128)S(1)} %get-tuple-element.118, bf16[32,128,256]{2,1,0:T(8,128)(2,1)S(1)} %select_convert_fusion.2), kind=kCustom, calls=%fused_computation.1.clone.1 | custom fusion | flops 1048576 | bytes 6291584 | tf_op jit(solution)/shard_map/while/body/scatter-add | solution.py:37
  165.1 0.1 compare_select_fusion.3
  165.2 5.4 gather_fusion
  170.6 0.7 add_compare_fusion.2
  171.2 2.6 select_convert_fusion.2
  173.9 9.2 %scatter_fusion = bf16[256,128,256]{2,1,0:T(8,128)(2,1)} fusion(bf16[256,128,256]{2,1,0:T(8,128)(2,1)} %get-tuple-element.133, s32[32]{0:T(128)S(1)} %get-tuple-element.118, bf16[32,128,256]{2,1,0:T(8,128)(2,1)S(1)} %select_convert_fusion.2), kind=kCustom, calls=%fused_computation.1.clone.1 | custom fusion | flops 1048576 | bytes 6291584 | tf_op jit(solution)/shard_map/while/body/scatter-add | solution.py:37
  183.1 0.0 reduce-scatter.2.cloned.1.call-update
  183.1 1.2 copy-done.1
  184.3 26.0 %all_to_all.10 = bf16[128,16,256]{2,1,0:T(8,128)(2,1)S(1)} all-to-all(bf16[128,16,256]{2,1,0:T(8,128)(2,1)S(1)} %bitcast.24), channel_id=1, replica_groups=mesh['row'=8,'col'=16] {'row','col'}, dimensions={0} | all-to-all | bytes 2097152 | tf_op jit(solution)/shard_map/all_to_all | solution.py:86
  210.3 117.8 %reduce-scatter.2.cloned.1.call-done = bf16[2048,256]{1,0:T(8,128)(2,1)} async-done(((bf16[32768,256]{1,0:T(8,128)(2,1)}), bf16[2048,256]{1,0:T(8,128)(2,1)}) %reduce-scatter.2.cloned.1.call-update) | async-done | bytes 1048592 | tf_op jit(solution)/shard_map/reduce_scatter | solution.py:71
  328.1 0.0 copy-done
  328.1 3.4 fusion.3
  331.5 6.7 %all-to-all-start = ((bf16[128,16,256]{2,1,0:T(8,128)(2,1)}), bf16[128,16,256]{2,1,0:T(8,128)(2,1)S(1)}, u32[]{:S(2)}, u32[]{:S(2)}) async-start(bf16[128,16,256]{2,1,0:T(8,128)(2,1)} %bitcast.6), calls=%async_computation.1 | async-start | bytes 2097152 | tf_op jit(solution)/shard_map/all_to_all | solution.py:78
  338.2 0.0 all-reduce.3.cloned.1.call-start
  338.2 0.0 copy-done.2
  338.2 1.2 fusion.4
  339.4 0.0 all-reduce.3.cloned.1.call-update
  339.4 0.0 all-reduce.5.cloned.1.call-start
  339.5 73.0 %all-reduce.3.cloned.1.call-done = f32[256,256]{1,0:T(8,128)} async-done(((f32[256,256]{1,0:T(8,128)}), f32[256,256]{1,0:T(8,128)}) %all-reduce.3.cloned.1.call-update) | async-done | bytes 262160 | tf_op jit(solution)/shard_map/psum | solution.py:12
  412.5 0.0 all-reduce.5.cloned.1.call-update
  412.6 144.8 %all-reduce.5.cloned.1.call-done = f32[256,256]{1,0:T(8,128)} async-done(((f32[256,256]{1,0:T(8,128)}), f32[256,256]{1,0:T(8,128)}) %all-reduce.5.cloned.1.call-update) | async-done | bytes 262160 | tf_op jit(solution)/shard_map/psum | solution.py:12
  557.3 1.7 broadcast_multiply_fusion
  559.0 0.0 all-to-all-done
  559.0 1.0 copy.20
  (7 shorter events, 0.0 us)
Async XLA Ops:
  7.2 321.0 %copy-start = (bf16[256,256]{1,0:T(8,128)(2,1)S(1)}, bf16[256,256]{1,0:T(8,128)(2,1)}, u32[]{:S(2)}) copy-start(bf16[256,256]{1,0:T(8,128)(2,1)} %param.10) | copy-start | bytes 393220
  7.2 97.6 %all-gather.2.cloned.1.call-start = ((), (), s32[]{:S(2)}) async-start(), calls=%async_computation.3 | async-start | bytes 9437184 | tf_op jit(solution)/shard_map/all_gather | solution.py:61
  7.9 320.2 %reduce-scatter.2.cloned.1.call-start = ((), (), s32[]{:S(2)}) async-start(), calls=%async_computation.4 | async-start | bytes 17825792 | tf_op jit(solution)/shard_map/reduce_scatter | solution.py:71
  104.8 6.0 %copy-start.3 = (s32[1,1,128]{2,1,0:T(1,128)S(1)}, s32[1,1,128]{2,1,0:T(1,128)}, u32[]{:S(2)}) copy-start(s32[1,1,128]{2,1,0:T(1,128)} %param.11) | copy-start | bytes 1540
  104.8 6.0 %copy-start.4 = (s32[1,1,128]{2,1,0:T(1,128)S(1)}, s32[1,1,128]{2,1,0:T(1,128)}, u32[]{:S(2)}) copy-start(s32[1,1,128]{2,1,0:T(1,128)} %param.12) | copy-start | bytes 1540
  183.1 1.2 copy-start.1
  331.5 6.7 %copy-start.2 = (bf16[2048,256]{1,0:T(8,128)(2,1)S(1)}, bf16[2048,256]{1,0:T(8,128)(2,1)}, u32[]{:S(2)}) copy-start(bf16[2048,256]{1,0:T(8,128)(2,1)} %reduce-scatter.2.cloned.1.call-done) | copy-start | bytes 3145732
  331.5 227.5 %all-to-all-start = ((bf16[128,16,256]{2,1,0:T(8,128)(2,1)}), bf16[128,16,256]{2,1,0:T(8,128)(2,1)S(1)}, u32[]{:S(2)}, u32[]{:S(2)}) async-start(bf16[128,16,256]{2,1,0:T(8,128)(2,1)} %bitcast.6), calls=%async_computation.1 | async-start | bytes 2097152 | tf_op jit(solution)/shard_map/all_to_all | solution.py:78
  338.2 74.4 %all-reduce.3.cloned.1.call-start = ((), (), s32[]{:S(2)}) async-start(), calls=%async_computation.5 | async-start | bytes 524288 | tf_op jit(solution)/shard_map/psum | solution.py:12
  339.4 217.9 %all-reduce.5.cloned.1.call-start = ((), (), s32[]{:S(2)}) async-start(), calls=%async_computation.6 | async-start | bytes 524288 | tf_op jit(solution)/shard_map/psum | solution.py:12
Sparse Core Ops, SparseCore 0:
  9.7 95.1 all-gather.1
  183.3 144.8 reduce-scatter.1
  342.1 70.4 all-reduce.2
  415.0 142.2 all-reduce.4
